TPU v7x, 32 devices: a whole 2x2x4 slice. The times are simulated.
32 devices in a mesh: rep: 4 (over y, x), fsdp: 4 (over z), ctx: 2 (over core).
Axes of the slice: x: 2, y: 2, z: 4, core: 2. Of those that a mesh axis runs over, the one named last changes fastest.
Arguments:
- inputs: bfloat16 [2, 16, 1024, 768], P(None, ('rep', 'fsdp'), 'ctx'), may hold values from -6 to 6
- weight_qkv: bfloat16 [768, 2304], P('fsdp'), may hold values from -0.21875 to 0.21875
- bias_query: bfloat16 [768], P('fsdp'), may hold values from -3 to 3
- bias_value: bfloat16 [768], P('fsdp'), may hold values from -3 to 3
- weight_mix: bfloat16 [768, 768], P('fsdp'), may hold values from -1.75 to 1.75
- bias_mix: bfloat16 [768], P('fsdp'), may hold values from -2 to 2
- gain_attn: bfloat16 [768], P('fsdp'), may hold values from 0.099609375 to 1.8984375
- shift_attn: bfloat16 [768], P('fsdp'), may hold values from -2 to 2
- gain_mlp: bfloat16 [768], P('fsdp'), may hold values from 0.099609375 to 1.8984375
- shift_mlp: bfloat16 [768], P('fsdp'), may hold values from -2 to 2
- weight_up: bfloat16 [768, 3072], P('fsdp'), may hold values from -0.21875 to 0.21875
- bias_up: bfloat16 [3072], P('fsdp'), may hold values from -3 to 3
- weight_down: bfloat16 [3072, 768], P('fsdp'), may hold values from -0.109375 to 0.109375
- bias_down: bfloat16 [768], P('fsdp'), may hold values from -2 to 2
- cotangent: bfloat16 [2, 16, 1024, 768], P(None, ('rep', 'fsdp'), 'ctx'), may hold values from -6 to 6
Outputs:
- outputs: bfloat16 [2, 16, 1024, 768], P(None, ('rep', 'fsdp'), 'ctx')
- grad_inputs: float32 [2, 16, 1024, 768], P(None, ('rep', 'fsdp'), 'ctx')
- weight_qkv_grad: float32 [768, 2304], P('fsdp')
- bias_query_grad: float32 [768], P('fsdp')
- bias_value_grad: float32 [768], P('fsdp')
- weight_mix_grad: float32 [768, 768], P('fsdp')
- bias_mix_grad: float32 [768], P('fsdp')
- gain_attn_grad: float32 [768], P('fsdp')
- shift_attn_grad: float32 [768], P('fsdp')
- gain_mlp_grad: float32 [768], P('fsdp')
- shift_mlp_grad: float32 [768], P('fsdp')
- weight_up_grad: float32 [768, 3072], P('fsdp')
- bias_up_grad: float32 [3072], P('fsdp')
- weight_down_grad: float32 [3072, 768], P('fsdp')
- bias_down_grad: float32 [768], P('fsdp')
All inputs are finite; a program needn't handle non-finite values.
Results may differ from a plain program's by a relative error of at most 0.018.
Values may be sent and summed in bfloat16 or wider, within the bound.
A program may use at most 320 MiB of HBM per device.

v0:
```python
from functools import partial
import jax
import jax.numpy as jnp
from jax import lax
from jax.sharding import PartitionSpec as P

H = 12
EPS = 1e-05


def from_behind(x, axis, by):
    peers = lax.axis_size(axis)
    pairs = [(i, i + by) for i in range(peers) if 0 <= i + by < peers]
    return lax.ppermute(x, axis, pairs)


def for_sending(x):

    def short(part):
        return part.astype(jnp.bfloat16) if part.dtype == jnp.float32 else part

    return jax.tree.map(short, x)


def norm_stats(values):
    center = values - jnp.mean(values, axis=-1, keepdims=True)
    inverse = lax.rsqrt(jnp.mean(center * center, axis=-1, keepdims=True) + EPS)
    return (center * inverse, inverse)


def norm_back(grad_norm, normal, inverse, gain):
    scaled = grad_norm * gain
    return inverse * (
        scaled
        - jnp.mean(scaled, axis=-1, keepdims=True)
        - normal * jnp.mean(scaled * normal, axis=-1, keepdims=True)
    )


def column_sum(values):
    return jnp.sum(values.astype(jnp.float32), axis=(0, 1))


def outer_sum(left, right):
    return jnp.einsum("sri,srj->ij", left, right, preferred_element_type=jnp.float32)


def project(left, weight):
    return jnp.einsum("sri,ij->srj", left, weight, preferred_element_type=jnp.float32)


def project_back(grad_rows, weight):
    return jnp.einsum("srj,ij->sri", grad_rows, weight, preferred_element_type=jnp.float32)


def split_heads(values):
    return values.reshape(values.shape[0], values.shape[1], H, values.shape[2] // H)


def attention_scores(query_heads, key_heads, allowed, factor):
    raw = jnp.einsum("sqhd,skhd->shqk", query_heads, key_heads, preferred_element_type=jnp.float32)
    return jnp.where(allowed, raw * factor, -1e30)


def local(
    inputs,
    weight_qkv,
    bias_query,
    bias_value,
    weight_mix,
    bias_mix,
    gain_attn,
    shift_attn,
    gain_mlp,
    shift_mlp,
    weight_up,
    bias_up,
    weight_down,
    bias_down,
    cotangent,
):
    shards = (
        weight_qkv,
        bias_query,
        bias_value,
        weight_mix,
        bias_mix,
        gain_attn,
        shift_attn,
        gain_mlp,
        shift_mlp,
        weight_up,
        bias_up,
        weight_down,
        bias_down,
    )
    width = weight_qkv.shape[1] // 3
    factor = (width // H) ** (-0.5)
    rows = inputs.shape[2]
    owners = lax.axis_size("fsdp")
    ctx_index = lax.axis_index("ctx")
    query_pos = lax.broadcasted_iota(jnp.int32, (rows, 2 * rows), 0)
    key_pos = lax.broadcasted_iota(jnp.int32, (rows, 2 * rows), 1) - rows
    allowed = (key_pos <= query_pos) & ((key_pos >= 0) | (ctx_index > 0))
    whole_zeros = tuple(
        (jnp.zeros((item.shape[0] * owners,) + item.shape[1:], jnp.float32) for item in shards)
    )
    bf16 = jnp.bfloat16
    f32 = jnp.float32

    def micro(totals, pair):
        tokens_in, grad_in = pair
        full = (
            lax.all_gather(shards[0], "fsdp", axis=0, tiled=True),
            lax.all_gather(shards[1], "fsdp", axis=0, tiled=True),
            lax.all_gather(shards[2], "fsdp", axis=0, tiled=True),
            lax.all_gather(shards[3], "fsdp", axis=0, tiled=True),
            lax.all_gather(shards[4], "fsdp", axis=0, tiled=True),
            lax.all_gather(shards[5], "fsdp", axis=0, tiled=True),
            lax.all_gather(shards[6], "fsdp", axis=0, tiled=True),
            lax.all_gather(shards[7], "fsdp", axis=0, tiled=True),
            lax.all_gather(shards[8], "fsdp", axis=0, tiled=True),
            lax.all_gather(shards[9], "fsdp", axis=0, tiled=True),
            lax.all_gather(shards[10], "fsdp", axis=0, tiled=True),
            lax.all_gather(shards[11], "fsdp", axis=0, tiled=True),
            lax.all_gather(shards[12], "fsdp", axis=0, tiled=True),
        )
        tokens = tokens_in.astype(f32)
        normal_one, inverse_one = norm_stats(tokens)
        first = (normal_one * full[5] + full[6]).astype(bf16)
        joined = project(first, full[0])
        query = (joined[..., :width] + full[1]).astype(bf16)
        key_own = joined[..., width : 2 * width].astype(bf16)
        value_own = (joined[..., 2 * width :] + full[2]).astype(bf16)
        key_prev, value_prev = from_behind((key_own, value_own), "ctx", 1)
        key_heads = split_heads(jnp.concatenate([key_prev, key_own], axis=1))
        value_heads = split_heads(jnp.concatenate([value_prev, value_own], axis=1))
        query_heads = split_heads(query)
        scores = attention_scores(query_heads, key_heads, allowed, factor)
        top = jnp.max(scores, axis=-1, keepdims=True)
        logsum = top + jnp.log(jnp.sum(jnp.exp(scores - top), axis=-1, keepdims=True))
        probs_low = jnp.exp(scores - logsum).astype(bf16)
        mixed = jnp.einsum("shqk,skhd->sqhd", probs_low, value_heads, preferred_element_type=f32)
        mixed = mixed.reshape(tokens.shape).astype(bf16)
        middle = tokens + project(mixed, full[3]) + full[4]
        normal_two, inverse_two = norm_stats(middle)
        second = (normal_two * full[7] + full[8]).astype(bf16)
        before = project(second, full[9]) + full[10]
        active = jax.nn.gelu(before, approximate=True).astype(bf16)
        result = (middle + project(active, full[11]) + full[12]).astype(bf16)
        again = (
            lax.all_gather(shards[0], "fsdp", axis=0, tiled=True),
            lax.all_gather(shards[1], "fsdp", axis=0, tiled=True),
            lax.all_gather(shards[2], "fsdp", axis=0, tiled=True),
            lax.all_gather(shards[3], "fsdp", axis=0, tiled=True),
            lax.all_gather(shards[4], "fsdp", axis=0, tiled=True),
            lax.all_gather(shards[5], "fsdp", axis=0, tiled=True),
            lax.all_gather(shards[6], "fsdp", axis=0, tiled=True),
            lax.all_gather(shards[7], "fsdp", axis=0, tiled=True),
            lax.all_gather(shards[8], "fsdp", axis=0, tiled=True),
            lax.all_gather(shards[9], "fsdp", axis=0, tiled=True),
            lax.all_gather(shards[10], "fsdp", axis=0, tiled=True),
            lax.all_gather(shards[11], "fsdp", axis=0, tiled=True),
            lax.all_gather(shards[12], "fsdp", axis=0, tiled=True),
        )
        grad_out = grad_in.astype(f32)
        d_down = grad_out.astype(bf16)
        g_wdown = outer_sum(active, d_down)
        g_bdown = column_sum(d_down)
        d_active = project_back(d_down, again[11])
        gelu_back = jax.vjp(partial(jax.nn.gelu, approximate=True), before)[1]
        d_before = gelu_back(d_active)[0].astype(bf16)
        g_wup = outer_sum(second, d_before)
        g_bup = column_sum(d_before)
        d_second = project_back(d_before, again[9])
        g_gmlp = jnp.sum(d_second * normal_two, axis=(0, 1))
        g_smlp = jnp.sum(d_second, axis=(0, 1))
        d_middle = grad_out + norm_back(d_second, normal_two, inverse_two, again[7])
        d_branch = d_middle.astype(bf16)
        g_wmix = outer_sum(mixed, d_branch)
        g_bmix = column_sum(d_branch)
        d_mixed = split_heads(project_back(d_branch, again[3]).astype(bf16))
        scores = attention_scores(query_heads, key_heads, allowed, factor)
        probs = jnp.exp(scores - logsum)
        probs_low = probs.astype(bf16)
        d_probs = jnp.einsum("sqhd,skhd->shqk", d_mixed, value_heads, preferred_element_type=f32)
        d_scores = (
            probs * (d_probs - jnp.sum(d_probs * probs, axis=-1, keepdims=True)) * factor
        ).astype(bf16)
        d_query = jnp.einsum("shqk,skhd->sqhd", d_scores, key_heads, preferred_element_type=f32)
        d_query = d_query.reshape(tokens.shape).astype(bf16)
        d_key_all = jnp.einsum("shqk,sqhd->skhd", d_scores, query_heads, preferred_element_type=f32)
        d_value_all = jnp.einsum("shqk,sqhd->skhd", probs_low, d_mixed, preferred_element_type=f32)
        d_key_all = d_key_all.reshape(tokens.shape[0], 2 * rows, width)
        d_value_all = d_value_all.reshape(tokens.shape[0], 2 * rows, width)
        key_back, value_back = (
            from_behind(d_key_all[:, :rows].astype(jnp.bfloat16), "ctx", -1).astype(jnp.float32),
            from_behind(d_value_all[:, :rows].astype(jnp.bfloat16), "ctx", -1).astype(jnp.float32),
        )
        d_key = (d_key_all[:, rows:] + key_back).astype(bf16)
        d_value = (d_value_all[:, rows:] + value_back).astype(bf16)
        d_joined = jnp.concatenate([d_query, d_key, d_value], axis=-1)
        g_wqkv = outer_sum(first, d_joined)
        g_bquery = column_sum(d_query)
        g_bvalue = column_sum(d_value)
        d_first = project_back(d_joined, again[0])
        g_gattn = jnp.sum(d_first * normal_one, axis=(0, 1))
        g_sattn = jnp.sum(d_first, axis=(0, 1))
        d_tokens = d_middle + norm_back(d_first, normal_one, inverse_one, again[5])
        terms = (
            g_wqkv,
            g_bquery,
            g_bvalue,
            g_wmix,
            g_bmix,
            g_gattn,
            g_sattn,
            g_gmlp,
            g_smlp,
            g_wup,
            g_bup,
            g_wdown,
            g_bdown,
        )
        totals = tuple((left + right for left, right in zip(totals, terms)))
        return (totals, (result, d_tokens))

    totals, (results, grad_tokens) = lax.scan(micro, whole_zeros, (inputs, cotangent))
    shares = jax.tree.map(
        lambda part: part.astype(jnp.float32),
        lax.psum_scatter(for_sending(totals), "fsdp", scatter_dimension=0, tiled=True),
    )
    summed = jax.tree.map(
        lambda part: part.astype(jnp.float32), lax.psum(for_sending(shares), ("rep", "ctx"))
    )
    return (results, grad_tokens) + tuple(summed)


def solution(mesh):
    in_specs = (
        P(None, ("rep", "fsdp"), "ctx", None),
        P("fsdp", None),
        P("fsdp"),
        P("fsdp"),
        P("fsdp", None),
        P("fsdp"),
        P("fsdp"),
        P("fsdp"),
        P("fsdp"),
        P("fsdp"),
        P("fsdp", None),
        P("fsdp"),
        P("fsdp", None),
        P("fsdp"),
        P(None, ("rep", "fsdp"), "ctx", None),
    )
    out_specs = (
        P(None, ("rep", "fsdp"), "ctx", None),
        P(None, ("rep", "fsdp"), "ctx", None),
        P("fsdp", None),
        P("fsdp"),
        P("fsdp"),
        P("fsdp", None),
        P("fsdp"),
        P("fsdp"),
        P("fsdp"),
        P("fsdp"),
        P("fsdp"),
        P("fsdp", None),
        P("fsdp"),
        P("fsdp", None),
        P("fsdp"),
    )
    return jax.shard_map(local, mesh=mesh, in_specs=in_specs, out_specs=out_specs, check_vma=False)
```

profile of v0, /device:TPU:0, one launch (start us, length us, event | category | flops | bytes accessed | tf_op | source)
XLA Modules:
  0.0 1352.4 jit_solution(5778753269937234375)
XLA Ops:
  8.2 974.8 %while.41 = (s32[]{:T(128)}, f32[768,2304]{1,0:T(8,128)}, f32[768]{0:T(1024)}, f32[768]{0:T(1024)}, f32[768,768]{1,0:T(8,128)}, /*index=5*/f32[768]{0:T(1024)}, ...) while((s32[]{:T(128)}, f32[768,2304]{1,0:T(8,128)}, ...), condition=%wide.region_21.22_spmd.clone, body=%wide.region_0.21_spmd.clone.sunk | while | flops 26950144000 | bytes 699213696 | solution.py:228
  19.6 21.4 %all-reduce.30 = (bf16[768]{0:T(1024)(128)(2,1)S(1)}, bf16[768]{0:T(1024)(128)(2,1)S(1)}, bf16[768]{0:T(1024)(128)(2,1)S(1)}, bf16[768]{0:T(1024)(128)(2,1)S(1)}...) all-reduce(bf16[768]{0:T(1024)(128)(2,1)S(1)} %dynamic-update-slice, ...), channel_id=1, replica_groups=mesh['rep'=4,'fsdp'=4,'ctx'=2] {'fsdp'}, use_global_device_ids=true, to_apply=%add.1 | all-reduce | flops 6144 | bytes 24576 | tf_op jit(solution)/shard_map/while
  42.7 41.6 %all-gather.11.cloned.1.call-done = bf16[768,2304]{1,0:T(8,128)(2,1)} async-done(((bf16[192,2304]{1,0:T(8,128)(2,1)}), bf16[768,2304]{1,0:T(8,128)(2,1)}) %all-gather.11.cloned.1.call-update) | async-done | bytes 3538960 | tf_op jit(solution)/shard_map/while/body/eval_jaxpr/all_gather | solution.py:114
  94.7 13.2 all-gather.3
  116.7 15.2 %fusion.201 = (f32[12,512]{1,0:T(8,128)S(1)}, f32[12,512,1024]{2,1,0:T(8,128)}) fusion(pred[512,1024]{1,0:T(8,128)(4,1)} %fusion.200, bf16[512,12,64]{0,2,1:T(8,128)(2,1)} %bitcast.212, bf16[1024,12,64]{0,2,1:T(8,128)(2,1)} %bitcast.210), kind=kOutput, calls=%fused_computation.8.clone.1 | convolution fusion | flops 824174592 | bytes 28073984 | tf_op jit(solution)/shard_map/while/body/eval_jaxpr/sqhd,skhd->shqk/dot_general | solution.py:61
  131.9 11.8 exponential_reduce_fusion.2
  143.8 12.1 convolution_convert_fusion.4
  158.9 46.3 %all-gather.13.cloned.1.call-done = bf16[768,3072]{1,0:T(8,128)(2,1)} async-done(((bf16[192,3072]{1,0:T(8,128)(2,1)}), bf16[768,3072]{1,0:T(8,128)(2,1)}) %all-gather.13.cloned.1.call-update) | async-done | bytes 4718608 | tf_op jit(solution)/shard_map/while/body/eval_jaxpr/all_gather | solution.py:123
  212.3 82.2 %all-gather.15.cloned.1.call-done = bf16[3072,768]{1,0:T(8,128)(2,1)} async-done(((bf16[768,768]{1,0:T(8,128)(2,1)}), bf16[3072,768]{1,0:T(8,128)(2,1)}) %all-gather.15.cloned.1.call-update) | async-done | bytes 4718608 | tf_op jit(solution)/shard_map/while/body/eval_jaxpr/all_gather | solution.py:163
  312.2 13.6 %fusion.204 = f32[12,64,1024]{2,1,0:T(8,128)} fusion(bf16[512,12,64]{0,2,1:T(8,128)(2,1)} %bitcast.208, f32[12,512]{1,0:T(8,128)S(1)} %log_add_fusion.2, f32[12,512,1024]{2,1,0:T(8,128)} %get-tuple-element.914, pred[512,1024]{1,0:T(8,128)(4,1)} %fusion.200), kind=kOutput, calls=%fused_computation.107.clone.1 | convolution fusion | flops 830472192 | bytes 29646848 | tf_op jit(solution)/shard_map/while/body/eval_jaxpr/shqk,sqhd->skhd/dot_general | solution.py:193
  335.9 52.3 %convert_reduce_fusion.16 = (f32[12,64]{1,0:T(8,128)S(1)}, bf16[12,64,512]{2,1,0:T(8,128)(2,1)}) fusion(bf16[1024,12,64]{0,2,1:T(8,128)(2,1)} %bitcast.211, f32[12,512,1024]{2,1,0:T(8,128)} %fusion.205, f32[12,512]{1,0:T(8,128)S(1)} %log_add_fusion.2, f32[12,512,1024]{2,1,0:T(8,128)} %get-tuple-element.914, pred[512,1024]{1,0:T(8,128)(4,1)} %fusion.200), kind=kOutput, calls=%fused_computation.77.clone.1 | convolution fusion | flops 875698432 | bytes 53242880 | tf_op jit(solution)/shard_map/while/body/eval_jaxpr/shqk,skhd->sqhd/dot_general | solution.py:190
  388.2 54.3 %fusion.206 = f32[12,64,1024]{2,1,0:T(8,128)} fusion(bf16[512,12,64]{0,2,1:T(8,128)(2,1)} %bitcast.213, f32[12,512,1024]{2,1,0:T(8,128)} %fusion.205, f32[12,512]{1,0:T(8,128)S(1)} %log_add_fusion.2, f32[12,512,1024]{2,1,0:T(8,128)} %get-tuple-element.914, pred[512,1024]{1,0:T(8,128)(4,1)} %fusion.200), kind=kOutput, calls=%fused_computation.10.clone.1 | convolution fusion | flops 874519552 | bytes 54812672 | tf_op jit(solution)/shard_map/while/body/eval_jaxpr/shqk,sqhd->skhd/dot_general | solution.py:192
  442.5 10.5 select_add_fusion.31
  502.7 16.6 %all-reduce.30 = (bf16[768]{0:T(1024)(128)(2,1)S(1)}, bf16[768]{0:T(1024)(128)(2,1)S(1)}, bf16[768]{0:T(1024)(128)(2,1)S(1)}, bf16[768]{0:T(1024)(128)(2,1)S(1)}...) all-reduce(bf16[768]{0:T(1024)(128)(2,1)S(1)} %dynamic-update-slice, ...), channel_id=1, replica_groups=mesh['rep'=4,'fsdp'=4,'ctx'=2] {'fsdp'}, use_global_device_ids=true, to_apply=%add.1 | all-reduce | flops 6144 | bytes 24576 | tf_op jit(solution)/shard_map/while
  521.0 43.7 %all-gather.11.cloned.1.call-done = bf16[768,2304]{1,0:T(8,128)(2,1)} async-done(((bf16[192,2304]{1,0:T(8,128)(2,1)}), bf16[768,2304]{1,0:T(8,128)(2,1)}) %all-gather.11.cloned.1.call-update) | async-done | bytes 3538960 | tf_op jit(solution)/shard_map/while/body/eval_jaxpr/all_gather | solution.py:114
  575.1 13.2 all-gather.3
  596.9 15.3 %fusion.201 = (f32[12,512]{1,0:T(8,128)S(1)}, f32[12,512,1024]{2,1,0:T(8,128)}) fusion(pred[512,1024]{1,0:T(8,128)(4,1)} %fusion.200, bf16[512,12,64]{0,2,1:T(8,128)(2,1)} %bitcast.212, bf16[1024,12,64]{0,2,1:T(8,128)(2,1)} %bitcast.210), kind=kOutput, calls=%fused_computation.8.clone.1 | convolution fusion | flops 824174592 | bytes 28073984 | tf_op jit(solution)/shard_map/while/body/eval_jaxpr/sqhd,skhd->shqk/dot_general | solution.py:61
  612.2 11.8 exponential_reduce_fusion.2
  624.0 12.1 convolution_convert_fusion.4
  639.1 46.4 %all-gather.13.cloned.1.call-done = bf16[768,3072]{1,0:T(8,128)(2,1)} async-done(((bf16[192,3072]{1,0:T(8,128)(2,1)}), bf16[768,3072]{1,0:T(8,128)(2,1)}) %all-gather.13.cloned.1.call-update) | async-done | bytes 4718608 | tf_op jit(solution)/shard_map/while/body/eval_jaxpr/all_gather | solution.py:123
  692.7 82.4 %all-gather.15.cloned.1.call-done = bf16[3072,768]{1,0:T(8,128)(2,1)} async-done(((bf16[768,768]{1,0:T(8,128)(2,1)}), bf16[3072,768]{1,0:T(8,128)(2,1)}) %all-gather.15.cloned.1.call-update) | async-done | bytes 4718608 | tf_op jit(solution)/shard_map/while/body/eval_jaxpr/all_gather | solution.py:163
  793.1 13.6 %fusion.204 = f32[12,64,1024]{2,1,0:T(8,128)} fusion(bf16[512,12,64]{0,2,1:T(8,128)(2,1)} %bitcast.208, f32[12,512]{1,0:T(8,128)S(1)} %log_add_fusion.2, f32[12,512,1024]{2,1,0:T(8,128)} %get-tuple-element.914, pred[512,1024]{1,0:T(8,128)(4,1)} %fusion.200), kind=kOutput, calls=%fused_computation.107.clone.1 | convolution fusion | flops 830472192 | bytes 29646848 | tf_op jit(solution)/shard_map/while/body/eval_jaxpr/shqk,sqhd->skhd/dot_general | solution.py:193
  816.8 52.3 %convert_reduce_fusion.16 = (f32[12,64]{1,0:T(8,128)S(1)}, bf16[12,64,512]{2,1,0:T(8,128)(2,1)}) fusion(bf16[1024,12,64]{0,2,1:T(8,128)(2,1)} %bitcast.211, f32[12,512,1024]{2,1,0:T(8,128)} %fusion.205, f32[12,512]{1,0:T(8,128)S(1)} %log_add_fusion.2, f32[12,512,1024]{2,1,0:T(8,128)} %get-tuple-element.914, pred[512,1024]{1,0:T(8,128)(4,1)} %fusion.200), kind=kOutput, calls=%fused_computation.77.clone.1 | convolution fusion | flops 875698432 | bytes 53242880 | tf_op jit(solution)/shard_map/while/body/eval_jaxpr/shqk,skhd->sqhd/dot_general | solution.py:190
  869.1 54.1 %fusion.206 = f32[12,64,1024]{2,1,0:T(8,128)} fusion(bf16[512,12,64]{0,2,1:T(8,128)(2,1)} %bitcast.213, f32[12,512,1024]{2,1,0:T(8,128)} %fusion.205, f32[12,512]{1,0:T(8,128)S(1)} %log_add_fusion.2, f32[12,512,1024]{2,1,0:T(8,128)} %get-tuple-element.914, pred[512,1024]{1,0:T(8,128)(4,1)} %fusion.200), kind=kOutput, calls=%fused_computation.10.clone.1 | convolution fusion | flops 874519552 | bytes 54812672 | tf_op jit(solution)/shard_map/while/body/eval_jaxpr/shqk,sqhd->skhd/dot_general | solution.py:192
  923.2 13.2 select_add_fusion.31
  1004.5 11.2 reduce-scatter.7.cloned.1.call-done
  1015.7 67.2 %reduce-scatter.5.cloned.1.call-done = bf16[192,2304]{1,0:T(8,128)(2,1)} async-done(((bf16[768,2304]{1,0:T(8,128)(2,1)}), bf16[192,2304]{1,0:T(8,128)(2,1)}) %reduce-scatter.5.cloned.1.call-update) | async-done | bytes 884752 | tf_op jit(solution)/shard_map/reduce_scatter | solution.py:231
  1082.9 87.5 %reduce-scatter.9.cloned.1.call-done = bf16[192,3072]{1,0:T(8,128)(2,1)} async-done(((bf16[768,3072]{1,0:T(8,128)(2,1)}), bf16[192,3072]{1,0:T(8,128)(2,1)}) %reduce-scatter.9.cloned.1.call-update) | async-done | bytes 1179664 | tf_op jit(solution)/shard_map/reduce_scatter | solution.py:231
  1170.4 88.0 %reduce-scatter.11.cloned.1.call-done = bf16[768,768]{1,0:T(8,128)(2,1)} async-done(((bf16[3072,768]{1,0:T(8,128)(2,1)}), bf16[768,768]{1,0:T(8,128)(2,1)}) %reduce-scatter.11.cloned.1.call-update) | async-done | bytes 1179664 | tf_op jit(solution)/shard_map/reduce_scatter | solution.py:231
  1260.5 18.3 %all-reduce.28 = (bf16[768]{0:T(1024)(128)(2,1)S(1)}, bf16[768]{0:T(1024)(128)(2,1)S(1)}, bf16[768]{0:T(1024)(128)(2,1)S(1)}, bf16[768]{0:T(1024)(128)(2,1)S(1)}...) all-reduce(bf16[768]{0:T(1024)(128)(2,1)S(1)} %convert_element_type, ...), channel_id=3, replica_groups=mesh['rep'=4,'fsdp'=4,'ctx'=2] {'fsdp'}, use_global_device_ids=true, to_apply=%region_24.25.clone | all-reduce | flops 9216 | bytes 36864
  1279.5 12.3 all-reduce.26
  1296.9 40.1 %all-reduce.33.cloned.1.call-done = (bf16[192,2304]{1,0:T(8,128)(2,1)}, bf16[192,768]{1,0:T(8,128)(2,1)}, bf16[192,3072]{1,0:T(8,128)(2,1)}, bf16[768,768]{1,0:T(8,128)(2,1)}) async-done(((bf16[192,2304]{1,0:T(8,128)(2,1)}, bf16[192,768]{1,0:T(8,128)(2,1)}, bf16[192,3072]{1,0:T(8,128)(2,1)}, bf16[768,768]{1,0:T(8,128)(2,1)}), (bf16[192,2304]{1,0:T(8,128)(2,1)}, bf16[192,768]{1,0:T(8,128)(2,1)}, ...) | async-done | bytes 3538960 | tf_op jit(solution)/shard_map/psum | solution.py:234
  (425 shorter events, 254.4 us)
Async XLA Ops:
  8.6 99.5 %copy-start.21 = (s32[1024]{0:T(1024)}, s32[1024]{0:T(1024)S(1)}, u32[]{:S(2)}) copy-start(s32[1024]{0:T(1024)S(1)} %get-tuple-element.1055) | copy-start | bytes 12292 | tf_op jit(solution)/shard_map/while
  8.6 99.5 %copy-start.41 = (pred[1024]{0:T(1024)(128)(4,1)}, pred[1024]{0:T(1024)(128)(4,1)S(1)}, u32[]{:S(2)}) copy-start(pred[1024]{0:T(1024)(128)(4,1)S(1)} %get-tuple-element.1056) | copy-start | bytes 3076 | tf_op jit(solution)/shard_map/while
  8.7 75.6 %all-gather.11.cloned.1.call-start = ((), (), s32[]{:S(2)}) async-start(), calls=%async_computation.10 | async-start | bytes 4423680 | tf_op jit(solution)/shard_map/while/body/eval_jaxpr/all_gather | solution.py:114
  9.4 146.5 %all-gather.9.cloned.1.call-start = ((), (), s32[]{:S(2)}) async-start(), calls=%async_computation.9 | async-start | bytes 1474560 | tf_op jit(solution)/shard_map/while/body/eval_jaxpr/all_gather | solution.py:117
  10.2 195.0 %all-gather.13.cloned.1.call-start = ((), (), s32[]{:S(2)}) async-start(), calls=%async_computation.11 | async-start | bytes 5898240 | tf_op jit(solution)/shard_map/while/body/eval_jaxpr/all_gather | solution.py:123
  10.9 283.6 %all-gather.15.cloned.1.call-start = ((), (), s32[]{:S(2)}) async-start(), calls=%async_computation.12 | async-start | bytes 5898240 | tf_op jit(solution)/shard_map/while/body/eval_jaxpr/all_gather | solution.py:163
  88.8 21.7 %collective-permute-start = (bf16[1,512,768]{2,1,0:T(8,128)(2,1)S(1)}, bf16[1,512,768]{2,1,0:T(8,128)(2,1)}, u32[]{:S(2)}, u32[]{:S(2)}) collective-permute-start(bf16[1,512,768]{2,1,0:T(8,128)(2,1)S(1)} %get-tuple-element.911), channel_id=1, source_target_pairs={{0,1},{2,3},{4,5},{6,7},{8,9},{10,11},{12,13},{14,15},{16,17},{18,... | collective-permute-start | bytes 2359304 | tf_op jit(solution)/shard_map/while/body/eval_jaxpr/ppermute | solution.py:14
  92.5 20.6 %collective-permute-start.1 = (bf16[1,512,768]{2,1,0:T(8,128)(2,1)}, bf16[1,512,768]{2,1,0:T(8,128)(2,1)}, u32[]{:S(2)}, u32[]{:S(2)}) collective-permute-start(bf16[1,512,768]{2,1,0:T(8,128)(2,1)} %slice.85), channel_id=1, source_target_pairs={{0,1},{2,3},{4,5},{6,7},{8,9},{10,11},{12,13},{14,15},{16,17},{18,... | collective-permute-start | bytes 2359304 | tf_op jit(solution)/shard_map/while/body/eval_jaxpr/ppermute | solution.py:14
  158.9 135.6 %copy-start.13 = (bf16[2,1,512,768]{3,2,1,0:T(8,128)(2,1)S(1)}, bf16[2,1,512,768]{3,2,1,0:T(8,128)(2,1)}, u32[]{:S(2)}) copy-start(bf16[2,1,512,768]{3,2,1,0:T(8,128)(2,1)} %get-tuple-element.1045) | copy-start | bytes 4718596 | tf_op jit(solution)/shard_map/while
  455.4 20.5 %collective-permute-start.2 = (bf16[1,512,768]{1,2,0:T(8,128)(2,1)}, bf16[1,512,768]{1,2,0:T(8,128)(2,1)}, u32[]{:S(2)}, u32[]{:S(2)}) collective-permute-start(bf16[1,512,768]{1,2,0:T(8,128)(2,1)} %slice.86), channel_id=1, source_target_pairs={{1,0},{3,2},{5,4},{7,6},{9,8},{11,10},{13,12},{15,14},{17,16},{19,... | collective-permute-start | bytes 2359304 | tf_op jit(solution)/shard_map/while/body/eval_jaxpr/ppermute | solution.py:14
  463.9 14.9 %collective-permute-start.3 = (bf16[1,512,768]{1,2,0:T(8,128)(2,1)S(1)}, bf16[1,512,768]{1,2,0:T(8,128)(2,1)S(1)}, u32[]{:S(2)}, u32[]{:S(2)}) collective-permute-start(bf16[1,512,768]{1,2,0:T(8,128)(2,1)S(1)} %slice.87), channel_id=1, source_target_pairs={{1,0},{3,2},{5,4},{7,6},{9,8},{11,10},{13,12},{15,14},{17,16},{19,... | collective-permute-start | bytes 2359304 | tf_op jit(solution)/shard_map/while/body/eval_jaxpr/ppermute | solution.py:14
  492.1 72.5 %all-gather.11.cloned.1.call-start = ((), (), s32[]{:S(2)}) async-start(), calls=%async_computation.10 | async-start | bytes 4423680 | tf_op jit(solution)/shard_map/while/body/eval_jaxpr/all_gather | solution.py:114
  492.7 143.5 %all-gather.9.cloned.1.call-start = ((), (), s32[]{:S(2)}) async-start(), calls=%async_computation.9 | async-start | bytes 1474560 | tf_op jit(solution)/shard_map/while/body/eval_jaxpr/all_gather | solution.py:117
  493.2 192.3 %all-gather.13.cloned.1.call-start = ((), (), s32[]{:S(2)}) async-start(), calls=%async_computation.11 | async-start | bytes 5898240 | tf_op jit(solution)/shard_map/while/body/eval_jaxpr/all_gather | solution.py:123
  494.0 281.0 %all-gather.15.cloned.1.call-start = ((), (), s32[]{:S(2)}) async-start(), calls=%async_computation.12 | async-start | bytes 5898240 | tf_op jit(solution)/shard_map/while/body/eval_jaxpr/all_gather | solution.py:163
  569.1 21.8 %collective-permute-start = (bf16[1,512,768]{2,1,0:T(8,128)(2,1)S(1)}, bf16[1,512,768]{2,1,0:T(8,128)(2,1)}, u32[]{:S(2)}, u32[]{:S(2)}) collective-permute-start(bf16[1,512,768]{2,1,0:T(8,128)(2,1)S(1)} %get-tuple-element.911), channel_id=1, source_target_pairs={{0,1},{2,3},{4,5},{6,7},{8,9},{10,11},{12,13},{14,15},{16,17},{18,... | collective-permute-start | bytes 2359304 | tf_op jit(solution)/shard_map/while/body/eval_jaxpr/ppermute | solution.py:14
  572.9 20.3 %collective-permute-start.1 = (bf16[1,512,768]{2,1,0:T(8,128)(2,1)}, bf16[1,512,768]{2,1,0:T(8,128)(2,1)}, u32[]{:S(2)}, u32[]{:S(2)}) collective-permute-start(bf16[1,512,768]{2,1,0:T(8,128)(2,1)} %slice.85), channel_id=1, source_target_pairs={{0,1},{2,3},{4,5},{6,7},{8,9},{10,11},{12,13},{14,15},{16,17},{18,... | collective-permute-start | bytes 2359304 | tf_op jit(solution)/shard_map/while/body/eval_jaxpr/ppermute | solution.py:14
  639.1 135.9 %copy-start.13 = (bf16[2,1,512,768]{3,2,1,0:T(8,128)(2,1)S(1)}, bf16[2,1,512,768]{3,2,1,0:T(8,128)(2,1)}, u32[]{:S(2)}) copy-start(bf16[2,1,512,768]{3,2,1,0:T(8,128)(2,1)} %get-tuple-element.1045) | copy-start | bytes 4718596 | tf_op jit(solution)/shard_map/while
  938.8 22.8 %collective-permute-start.2 = (bf16[1,512,768]{1,2,0:T(8,128)(2,1)}, bf16[1,512,768]{1,2,0:T(8,128)(2,1)}, u32[]{:S(2)}, u32[]{:S(2)}) collective-permute-start(bf16[1,512,768]{1,2,0:T(8,128)(2,1)} %slice.86), channel_id=1, source_target_pairs={{1,0},{3,2},{5,4},{7,6},{9,8},{11,10},{13,12},{15,14},{17,16},{19,... | collective-permute-start | bytes 2359304 | tf_op jit(solution)/shard_map/while/body/eval_jaxpr/ppermute | solution.py:14
  949.6 15.0 %collective-permute-start.3 = (bf16[1,512,768]{1,2,0:T(8,128)(2,1)S(1)}, bf16[1,512,768]{1,2,0:T(8,128)(2,1)S(1)}, u32[]{:S(2)}, u32[]{:S(2)}) collective-permute-start(bf16[1,512,768]{1,2,0:T(8,128)(2,1)S(1)} %slice.87), channel_id=1, source_target_pairs={{1,0},{3,2},{5,4},{7,6},{9,8},{11,10},{13,12},{15,14},{17,16},{19,... | collective-permute-start | bytes 2359304 | tf_op jit(solution)/shard_map/while/body/eval_jaxpr/ppermute | solution.py:14
  983.0 32.7 %reduce-scatter.7.cloned.1.call-start = ((), (), s32[]{:S(2)}) async-start(), calls=%async_computation.5 | async-start | bytes 1474560 | tf_op jit(solution)/shard_map/reduce_scatter | solution.py:231
  985.9 97.0 %reduce-scatter.5.cloned.1.call-start = ((), (), s32[]{:S(2)}) async-start(), calls=%async_computation.4 | async-start | bytes 4423680 | tf_op jit(solution)/shard_map/reduce_scatter | solution.py:231
  991.1 179.3 %reduce-scatter.9.cloned.1.call-start = ((), (), s32[]{:S(2)}) async-start(), calls=%async_computation.6 | async-start | bytes 5898240 | tf_op jit(solution)/shard_map/reduce_scatter | solution.py:231
  998.0 260.5 %reduce-scatter.11.cloned.1.call-start = ((), (), s32[]{:S(2)}) async-start(), calls=%async_computation.7 | async-start | bytes 5898240 | tf_op jit(solution)/shard_map/reduce_scatter | solution.py:231
  1004.4 254.1 %copy-start.49 = (u32[32]{0:T(128)S(1)}, u32[32]{0:T(128)}, u32[]{:S(2)}) copy-start(u32[32]{0:T(128)} %get-tuple-element.1116) | copy-start | bytes 388
  1004.4 256.0 %copy-start.39 = (f32[768]{0:T(1024)S(1)}, f32[768]{0:T(1024)}, u32[]{:S(2)}) copy-start(f32[768]{0:T(1024)} %get-tuple-element.421) | copy-start | bytes 9220
  1004.4 256.0 %copy-start.36 = (f32[768]{0:T(1024)S(1)}, f32[768]{0:T(1024)}, u32[]{:S(2)}) copy-start(f32[768]{0:T(1024)} %get-tuple-element.422) | copy-start | bytes 9220
  1004.4 256.0 %copy-start.33 = (f32[768]{0:T(1024)S(1)}, f32[768]{0:T(1024)}, u32[]{:S(2)}) copy-start(f32[768]{0:T(1024)} %get-tuple-element.424) | copy-start | bytes 9220
  1004.4 256.0 %copy-start.30 = (f32[768]{0:T(1024)S(1)}, f32[768]{0:T(1024)}, u32[]{:S(2)}) copy-start(f32[768]{0:T(1024)} %get-tuple-element.425) | copy-start | bytes 9220
  1004.4 256.1 %copy-start.27 = (f32[768]{0:T(1024)S(1)}, f32[768]{0:T(1024)}, u32[]{:S(2)}) copy-start(f32[768]{0:T(1024)} %get-tuple-element.426) | copy-start | bytes 9220
  1004.4 256.1 %copy-start.20 = (f32[3072]{0:T(1024)S(1)}, f32[3072]{0:T(1024)}, u32[]{:S(2)}) copy-start(f32[3072]{0:T(1024)} %get-tuple-element.430) | copy-start | bytes 36868
  1004.5 332.5 %all-reduce.33.cloned.1.call-start = ((), (), s32[]{:S(2)}) async-start(), calls=%async_computation.8 | async-start | bytes 7077888 | tf_op jit(solution)/shard_map/psum | solution.py:234
  (80 other events, 710.4 us)
Sparse Core Ops, SparseCore 0:
  11.1 73.1 all-gather.10
  85.9 29.1 all-gather.8
  116.6 88.5 all-gather.12
  206.6 87.8 all-gather.14
  494.2 70.3 all-gather.10
  566.0 29.3 all-gather.8
  597.0 88.5 all-gather.12
  687.1 87.8 all-gather.14
Sparse Core Ops, SparseCore 1:
  986.4 29.2 reduce-scatter.6
  1017.9 65.0 reduce-scatter.4
  1085.1 85.3 reduce-scatter.8
  1172.8 85.6 reduce-scatter.10
  1262.2 74.7 all-reduce.32
where the time goes:
time: 1360 us; the launch traced here: 1350 us
  waiting for transfers between devices  640 us (47%)
  matrix products  452 us (33%)
  blocking collectives  94.9 us (7%)
  other arithmetic  79.7 us (6%)
  local copies, waits for them, and re-layouts  45.7 us (3%)
  between operations  17.5 us (1%)
  starting transfers between devices  15.6 us (1%)
    reduce_scatter x4, waiting for transfers between devices, local(): lax.psum_scatter(for_sending(totals), 'fsdp', scatter_dimension=0, tiled=...  254 us
    all_gather x2, waiting for transfers between devices, micro(): lax.all_gather(shards[11], 'fsdp', axis=0, tiled=True)  165 us
    dot_general x2, matrix products, micro(): jnp.einsum('shqk,sqhd->skhd', d_scores, query_heads, preferred_element_ty...  108 us
    dot_general x2, matrix products, micro(): jnp.einsum('shqk,skhd->sqhd', d_scores, key_heads, preferred_element_type...  105 us
    all_gather x2, waiting for transfers between devices, micro(): lax.all_gather(shards[9], 'fsdp', axis=0, tiled=True)  92.7 us
    all_gather x2, waiting for transfers between devices, micro(): lax.all_gather(shards[0], 'fsdp', axis=0, tiled=True)  85.2 us
    dot_general x8, matrix products, outer_sum(): jnp.einsum('sri,srj->ij', left, right, preferred_element_type=jnp.float32)  56.7 us
    dot_general x8, matrix products, project(): jnp.einsum('sri,ij->srj', left, weight, preferred_element_type=jnp.float32)  46.1 us
  transfers between devices with their start and end apart: 21, of which 11 were waited for; matrix products, arithmetic and copies ran while one was open for 16% of the time, Pallas kernels for 0%

commit v1 on v0

--- a/solution.py
+++ b/solution.py
@@ -231,7 +231,7 @@
         lax.psum_scatter(for_sending(totals), "fsdp", scatter_dimension=0, tiled=True),
     )
     summed = jax.tree.map(
-        lambda part: part.astype(jnp.float32), lax.psum(for_sending(shares), ("rep", "ctx"))
+        lambda part: part.astype(jnp.float32), lax.psum(lax.psum(for_sending(shares), "ctx"), "rep")
     )
     return (results, grad_tokens) + tuple(summed)
 

time: 1360 us -> 1400 us (1.029)
  waiting for transfers between devices: 640 us -> 687 us
    psum x1 -> x2, waiting for transfers between devices: 40.1 us -> 86.4 us  [the longest x1 59.5 us: local(): lax.psum(lax.psum(for_sending(shares), 'ctx'), 'rep')]
  transfers between devices with their start and end apart: 21 -> 22, of which waited for: 11 -> 12; matrix products, arithmetic and copies ran while one was open for 16% -> 15% of each run, Pallas kernels for 0% -> 0%
where the time goes in v1:
time: 1400 us
  waiting for transfers between devices  687 us (49%)
  matrix products  452 us (32%)
  blocking collectives  96.5 us (7%)
  other arithmetic  79.7 us (6%)
  local copies, waits for them, and re-layouts  45.7 us (3%)
  between operations  17.4 us (1%)
  starting transfers between devices  15.5 us (1%)
    reduce_scatter x4, waiting for transfers between devices, local(): lax.psum_scatter(for_sending(totals), 'fsdp', scatter_dimension=0, tiled=...  254 us
    all_gather x2, waiting for transfers between devices, micro(): lax.all_gather(shards[11], 'fsdp', axis=0, tiled=True)  165 us
    dot_general x2, matrix products, micro(): jnp.einsum('shqk,sqhd->skhd', d_scores, query_heads, preferred_element_ty...  108 us
    dot_general x2, matrix products, micro(): jnp.einsum('shqk,skhd->sqhd', d_scores, key_heads, preferred_element_type...  105 us
    all_gather x2, waiting for transfers between devices, micro(): lax.all_gather(shards[9], 'fsdp', axis=0, tiled=True)  93.1 us
    all_gather x2, waiting for transfers between devices, micro(): lax.all_gather(shards[0], 'fsdp', axis=0, tiled=True)  85.2 us
    psum x1, waiting for transfers between devices, local(): lax.psum(lax.psum(for_sending(shares), 'ctx'), 'rep')  59.5 us
    dot_general x8, matrix products, outer_sum(): jnp.einsum('sri,srj->ij', left, right, preferred_element_type=jnp.float32)  56.8 us
  transfers between devices with their start and end apart: 22, of which 12 were waited for; matrix products, arithmetic and copies ran while one was open for 15% of the time, Pallas kernels for 0%

profile of v1, /device:TPU:0, one launch (start us, length us, event | category | flops | bytes accessed | tf_op | source)
XLA Modules:
  0.0 1401.1 jit_solution(9024046655045988966)
XLA Ops:
  8.2 975.7 %while.41 = (s32[]{:T(128)}, f32[768,2304]{1,0:T(8,128)}, f32[768]{0:T(1024)}, f32[768]{0:T(1024)}, f32[768,768]{1,0:T(8,128)}, /*index=5*/f32[768]{0:T(1024)}, ...) while((s32[]{:T(128)}, f32[768,2304]{1,0:T(8,128)}, ...), condition=%wide.region_21.22_spmd.clone, body=%wide.region_0.21_spmd.clone.sunk | while | flops 26950144000 | bytes 699213696 | solution.py:228
  19.6 21.5 %all-reduce.32 = (bf16[768]{0:T(1024)(128)(2,1)S(1)}, bf16[768]{0:T(1024)(128)(2,1)S(1)}, bf16[768]{0:T(1024)(128)(2,1)S(1)}, bf16[768]{0:T(1024)(128)(2,1)S(1)}...) all-reduce(bf16[768]{0:T(1024)(128)(2,1)S(1)} %dynamic-update-slice, ...), channel_id=1, replica_groups=mesh['rep'=4,'fsdp'=4,'ctx'=2] {'fsdp'}, use_global_device_ids=true, to_apply=%add.1 | all-reduce | flops 6144 | bytes 24576 | tf_op jit(solution)/shard_map/while
  42.8 41.6 %all-gather.11.cloned.1.call-done = bf16[768,2304]{1,0:T(8,128)(2,1)} async-done(((bf16[192,2304]{1,0:T(8,128)(2,1)}), bf16[768,2304]{1,0:T(8,128)(2,1)}) %all-gather.11.cloned.1.call-update) | async-done | bytes 3538960 | tf_op jit(solution)/shard_map/while/body/eval_jaxpr/all_gather | solution.py:114
  94.8 13.2 all-gather.3
  116.8 15.3 %fusion.201 = (f32[12,512]{1,0:T(8,128)S(1)}, f32[12,512,1024]{2,1,0:T(8,128)}) fusion(pred[512,1024]{1,0:T(8,128)(4,1)} %fusion.200, bf16[512,12,64]{0,2,1:T(8,128)(2,1)} %bitcast.212, bf16[1024,12,64]{0,2,1:T(8,128)(2,1)} %bitcast.210), kind=kOutput, calls=%fused_computation.8.clone.1 | convolution fusion | flops 824174592 | bytes 28073984 | tf_op jit(solution)/shard_map/while/body/eval_jaxpr/sqhd,skhd->shqk/dot_general | solution.py:61
  132.0 11.8 exponential_reduce_fusion.2
  143.9 12.1 convolution_convert_fusion.4
  159.0 46.4 %all-gather.13.cloned.1.call-done = bf16[768,3072]{1,0:T(8,128)(2,1)} async-done(((bf16[192,3072]{1,0:T(8,128)(2,1)}), bf16[768,3072]{1,0:T(8,128)(2,1)}) %all-gather.13.cloned.1.call-update) | async-done | bytes 4718608 | tf_op jit(solution)/shard_map/while/body/eval_jaxpr/all_gather | solution.py:123
  212.5 82.3 %all-gather.15.cloned.1.call-done = bf16[3072,768]{1,0:T(8,128)(2,1)} async-done(((bf16[768,768]{1,0:T(8,128)(2,1)}), bf16[3072,768]{1,0:T(8,128)(2,1)}) %all-gather.15.cloned.1.call-update) | async-done | bytes 4718608 | tf_op jit(solution)/shard_map/while/body/eval_jaxpr/all_gather | solution.py:163
  312.5 13.6 fusion.204
  336.2 52.4 %convert_reduce_fusion.16 = (f32[12,64]{1,0:T(8,128)S(1)}, bf16[12,64,512]{2,1,0:T(8,128)(2,1)}) fusion(bf16[1024,12,64]{0,2,1:T(8,128)(2,1)} %bitcast.211, f32[12,512,1024]{2,1,0:T(8,128)} %fusion.205, f32[12,512]{1,0:T(8,128)S(1)} %log_add_fusion.2, f32[12,512,1024]{2,1,0:T(8,128)} %get-tuple-element.927, pred[512,1024]{1,0:T(8,128)(4,1)} %fusion.200), kind=kOutput, calls=%fused_computation.77.clone.1 | convolution fusion | flops 875698432 | bytes 53242880 | tf_op jit(solution)/shard_map/while/body/eval_jaxpr/shqk,skhd->sqhd/dot_general | solution.py:190
  388.6 54.2 %fusion.206 = f32[12,64,1024]{2,1,0:T(8,128)} fusion(bf16[512,12,64]{0,2,1:T(8,128)(2,1)} %bitcast.213, f32[12,512,1024]{2,1,0:T(8,128)} %fusion.205, f32[12,512]{1,0:T(8,128)S(1)} %log_add_fusion.2, f32[12,512,1024]{2,1,0:T(8,128)} %get-tuple-element.927, pred[512,1024]{1,0:T(8,128)(4,1)} %fusion.200), kind=kOutput, calls=%fused_computation.10.clone.1 | convolution fusion | flops 874519552 | bytes 54812672 | tf_op jit(solution)/shard_map/while/body/eval_jaxpr/shqk,sqhd->skhd/dot_general | solution.py:192
  442.8 10.5 select_add_fusion.31
  503.0 16.6 %all-reduce.32 = (bf16[768]{0:T(1024)(128)(2,1)S(1)}, bf16[768]{0:T(1024)(128)(2,1)S(1)}, bf16[768]{0:T(1024)(128)(2,1)S(1)}, bf16[768]{0:T(1024)(128)(2,1)S(1)}...) all-reduce(bf16[768]{0:T(1024)(128)(2,1)S(1)} %dynamic-update-slice, ...), channel_id=1, replica_groups=mesh['rep'=4,'fsdp'=4,'ctx'=2] {'fsdp'}, use_global_device_ids=true, to_apply=%add.1 | all-reduce | flops 6144 | bytes 24576 | tf_op jit(solution)/shard_map/while
  521.3 43.7 %all-gather.11.cloned.1.call-done = bf16[768,2304]{1,0:T(8,128)(2,1)} async-done(((bf16[192,2304]{1,0:T(8,128)(2,1)}), bf16[768,2304]{1,0:T(8,128)(2,1)}) %all-gather.11.cloned.1.call-update) | async-done | bytes 3538960 | tf_op jit(solution)/shard_map/while/body/eval_jaxpr/all_gather | solution.py:114
  575.5 13.2 all-gather.3
  597.2 15.3 %fusion.201 = (f32[12,512]{1,0:T(8,128)S(1)}, f32[12,512,1024]{2,1,0:T(8,128)}) fusion(pred[512,1024]{1,0:T(8,128)(4,1)} %fusion.200, bf16[512,12,64]{0,2,1:T(8,128)(2,1)} %bitcast.212, bf16[1024,12,64]{0,2,1:T(8,128)(2,1)} %bitcast.210), kind=kOutput, calls=%fused_computation.8.clone.1 | convolution fusion | flops 824174592 | bytes 28073984 | tf_op jit(solution)/shard_map/while/body/eval_jaxpr/sqhd,skhd->shqk/dot_general | solution.py:61
  612.5 11.8 exponential_reduce_fusion.2
  624.4 12.1 convolution_convert_fusion.4
  639.5 46.7 %all-gather.13.cloned.1.call-done = bf16[768,3072]{1,0:T(8,128)(2,1)} async-done(((bf16[192,3072]{1,0:T(8,128)(2,1)}), bf16[768,3072]{1,0:T(8,128)(2,1)}) %all-gather.13.cloned.1.call-update) | async-done | bytes 4718608 | tf_op jit(solution)/shard_map/while/body/eval_jaxpr/all_gather | solution.py:123
  693.3 82.5 %all-gather.15.cloned.1.call-done = bf16[3072,768]{1,0:T(8,128)(2,1)} async-done(((bf16[768,768]{1,0:T(8,128)(2,1)}), bf16[3072,768]{1,0:T(8,128)(2,1)}) %all-gather.15.cloned.1.call-update) | async-done | bytes 4718608 | tf_op jit(solution)/shard_map/while/body/eval_jaxpr/all_gather | solution.py:163
  793.8 13.6 fusion.204
  817.5 52.3 %convert_reduce_fusion.16 = (f32[12,64]{1,0:T(8,128)S(1)}, bf16[12,64,512]{2,1,0:T(8,128)(2,1)}) fusion(bf16[1024,12,64]{0,2,1:T(8,128)(2,1)} %bitcast.211, f32[12,512,1024]{2,1,0:T(8,128)} %fusion.205, f32[12,512]{1,0:T(8,128)S(1)} %log_add_fusion.2, f32[12,512,1024]{2,1,0:T(8,128)} %get-tuple-element.927, pred[512,1024]{1,0:T(8,128)(4,1)} %fusion.200), kind=kOutput, calls=%fused_computation.77.clone.1 | convolution fusion | flops 875698432 | bytes 53242880 | tf_op jit(solution)/shard_map/while/body/eval_jaxpr/shqk,skhd->sqhd/dot_general | solution.py:190
  869.8 54.0 %fusion.206 = f32[12,64,1024]{2,1,0:T(8,128)} fusion(bf16[512,12,64]{0,2,1:T(8,128)(2,1)} %bitcast.213, f32[12,512,1024]{2,1,0:T(8,128)} %fusion.205, f32[12,512]{1,0:T(8,128)S(1)} %log_add_fusion.2, f32[12,512,1024]{2,1,0:T(8,128)} %get-tuple-element.927, pred[512,1024]{1,0:T(8,128)(4,1)} %fusion.200), kind=kOutput, calls=%fused_computation.10.clone.1 | convolution fusion | flops 874519552 | bytes 54812672 | tf_op jit(solution)/shard_map/while/body/eval_jaxpr/shqk,sqhd->skhd/dot_general | solution.py:192
  923.9 13.3 select_add_fusion.31
  1005.3 11.2 reduce-scatter.7.cloned.1.call-done
  1016.6 67.2 %reduce-scatter.5.cloned.1.call-done = bf16[192,2304]{1,0:T(8,128)(2,1)} async-done(((bf16[768,2304]{1,0:T(8,128)(2,1)}), bf16[192,2304]{1,0:T(8,128)(2,1)}) %reduce-scatter.5.cloned.1.call-update) | async-done | bytes 884752 | tf_op jit(solution)/shard_map/reduce_scatter | solution.py:231
  1083.8 87.5 %reduce-scatter.9.cloned.1.call-done = bf16[192,3072]{1,0:T(8,128)(2,1)} async-done(((bf16[768,3072]{1,0:T(8,128)(2,1)}), bf16[192,3072]{1,0:T(8,128)(2,1)}) %reduce-scatter.9.cloned.1.call-update) | async-done | bytes 1179664 | tf_op jit(solution)/shard_map/reduce_scatter | solution.py:231
  1171.3 88.0 %reduce-scatter.11.cloned.1.call-done = bf16[768,768]{1,0:T(8,128)(2,1)} async-done(((bf16[3072,768]{1,0:T(8,128)(2,1)}), bf16[768,768]{1,0:T(8,128)(2,1)}) %reduce-scatter.11.cloned.1.call-update) | async-done | bytes 1179664 | tf_op jit(solution)/shard_map/reduce_scatter | solution.py:231
  1259.4 26.9 %all-reduce.38.cloned.1.call-done = (bf16[192,2304]{1,0:T(8,128)(2,1)}, bf16[192,768]{1,0:T(8,128)(2,1)}, bf16[192,3072]{1,0:T(8,128)(2,1)}, bf16[768,768]{1,0:T(8,128)(2,1)}) async-done(((bf16[192,2304]{1,0:T(8,128)(2,1)}, bf16[192,768]{1,0:T(8,128)(2,1)}, bf16[192,3072]{1,0:T(8,128)(2,1)}, bf16[768,768]{1,0:T(8,128)(2,1)}), (bf16[192,2304]{1,0:T(8,128)(2,1)}, bf16[192,768]{1,0:T(8,128)(2,1)}, ...) | async-done | bytes 3538960 | tf_op jit(solution)/shard_map/psum | solution.py:234
  1288.4 19.2 %all-reduce.26 = (bf16[768]{0:T(1024)(128)(2,1)S(1)}, bf16[768]{0:T(1024)(128)(2,1)S(1)}, bf16[768]{0:T(1024)(128)(2,1)S(1)}, bf16[768]{0:T(1024)(128)(2,1)S(1)}...) all-reduce(bf16[768]{0:T(1024)(128)(2,1)S(1)} %convert_element_type, ...), channel_id=3, replica_groups=mesh['rep'=4,'fsdp'=4,'ctx'=2] {'fsdp'}, use_global_device_ids=true, to_apply=%region_25.26.clone | all-reduce | flops 9216 | bytes 36864
  1326.2 59.5 %all-reduce.36.cloned.1.call-done = (bf16[192,2304]{1,0:T(8,128)(2,1)}, bf16[192,768]{1,0:T(8,128)(2,1)}, bf16[192,3072]{1,0:T(8,128)(2,1)}, bf16[768,768]{1,0:T(8,128)(2,1)}) async-done(((bf16[192,2304]{1,0:T(8,128)(2,1)}, bf16[192,768]{1,0:T(8,128)(2,1)}, bf16[192,3072]{1,0:T(8,128)(2,1)}, bf16[768,768]{1,0:T(8,128)(2,1)}), (bf16[192,2304]{1,0:T(8,128)(2,1)}, bf16[192,768]{1,0:T(8,128)(2,1)}, ...) | async-done | bytes 3538960 | tf_op jit(solution)/shard_map/psum | solution.py:234
  (429 shorter events, 267.1 us)
Async XLA Ops:
  8.6 99.6 %copy-start.21 = (s32[1024]{0:T(1024)}, s32[1024]{0:T(1024)S(1)}, u32[]{:S(2)}) copy-start(s32[1024]{0:T(1024)S(1)} %get-tuple-element.1068) | copy-start | bytes 12292 | tf_op jit(solution)/shard_map/while
  8.6 99.6 %copy-start.41 = (pred[1024]{0:T(1024)(128)(4,1)}, pred[1024]{0:T(1024)(128)(4,1)S(1)}, u32[]{:S(2)}) copy-start(pred[1024]{0:T(1024)(128)(4,1)S(1)} %get-tuple-element.1069) | copy-start | bytes 3076 | tf_op jit(solution)/shard_map/while
  8.7 33.8 %copy-start.4 = (bf16[2,1,512,768]{3,2,1,0:T(8,128)(2,1)S(1)}, bf16[2,1,512,768]{3,2,1,0:T(8,128)(2,1)}, u32[]{:S(2)}) copy-start(bf16[2,1,512,768]{3,2,1,0:T(8,128)(2,1)} %get-tuple-element.1053) | copy-start | bytes 4718596 | tf_op jit(solution)/shard_map/while
  8.7 75.7 %all-gather.11.cloned.1.call-start = ((), (), s32[]{:S(2)}) async-start(), calls=%async_computation.11 | async-start | bytes 4423680 | tf_op jit(solution)/shard_map/while/body/eval_jaxpr/all_gather | solution.py:114
  9.4 146.6 %all-gather.9.cloned.1.call-start = ((), (), s32[]{:S(2)}) async-start(), calls=%async_computation.10 | async-start | bytes 1474560 | tf_op jit(solution)/shard_map/while/body/eval_jaxpr/all_gather | solution.py:117
  10.2 195.2 %all-gather.13.cloned.1.call-start = ((), (), s32[]{:S(2)}) async-start(), calls=%async_computation.12 | async-start | bytes 5898240 | tf_op jit(solution)/shard_map/while/body/eval_jaxpr/all_gather | solution.py:123
  10.9 283.9 %all-gather.15.cloned.1.call-start = ((), (), s32[]{:S(2)}) async-start(), calls=%async_computation.13 | async-start | bytes 5898240 | tf_op jit(solution)/shard_map/while/body/eval_jaxpr/all_gather | solution.py:163
  88.9 21.7 %collective-permute-start = (bf16[1,512,768]{2,1,0:T(8,128)(2,1)S(1)}, bf16[1,512,768]{2,1,0:T(8,128)(2,1)}, u32[]{:S(2)}, u32[]{:S(2)}) collective-permute-start(bf16[1,512,768]{2,1,0:T(8,128)(2,1)S(1)} %get-tuple-element.924), channel_id=1, source_target_pairs={{0,1},{2,3},{4,5},{6,7},{8,9},{10,11},{12,13},{14,15},{16,17},{18,... | collective-permute-start | bytes 2359304 | tf_op jit(solution)/shard_map/while/body/eval_jaxpr/ppermute | solution.py:14
  92.5 20.6 %collective-permute-start.1 = (bf16[1,512,768]{2,1,0:T(8,128)(2,1)}, bf16[1,512,768]{2,1,0:T(8,128)(2,1)}, u32[]{:S(2)}, u32[]{:S(2)}) collective-permute-start(bf16[1,512,768]{2,1,0:T(8,128)(2,1)} %slice.85), channel_id=1, source_target_pairs={{0,1},{2,3},{4,5},{6,7},{8,9},{10,11},{12,13},{14,15},{16,17},{18,... | collective-permute-start | bytes 2359304 | tf_op jit(solution)/shard_map/while/body/eval_jaxpr/ppermute | solution.py:14
  113.1 30.8 %copy-start = (bf16[1,1024,768]{1,2,0:T(8,128)(2,1)}, bf16[1,1024,768]{1,2,0:T(8,128)(2,1)S(1)}, u32[]{:S(2)}) copy-start(bf16[1,1024,768]{1,2,0:T(8,128)(2,1)S(1)} %copy.50) | copy-start | bytes 4718596 | tf_op jit(solution)/shard_map/while
  159.0 135.8 %copy-start.13 = (bf16[2,1,512,768]{3,2,1,0:T(8,128)(2,1)S(1)}, bf16[2,1,512,768]{3,2,1,0:T(8,128)(2,1)}, u32[]{:S(2)}) copy-start(bf16[2,1,512,768]{3,2,1,0:T(8,128)(2,1)} %get-tuple-element.1058) | copy-start | bytes 4718596 | tf_op jit(solution)/shard_map/while
  455.7 20.5 %collective-permute-start.2 = (bf16[1,512,768]{1,2,0:T(8,128)(2,1)}, bf16[1,512,768]{1,2,0:T(8,128)(2,1)}, u32[]{:S(2)}, u32[]{:S(2)}) collective-permute-start(bf16[1,512,768]{1,2,0:T(8,128)(2,1)} %slice.86), channel_id=1, source_target_pairs={{1,0},{3,2},{5,4},{7,6},{9,8},{11,10},{13,12},{15,14},{17,16},{19,... | collective-permute-start | bytes 2359304 | tf_op jit(solution)/shard_map/while/body/eval_jaxpr/ppermute | solution.py:14
  464.2 14.9 %collective-permute-start.3 = (bf16[1,512,768]{1,2,0:T(8,128)(2,1)S(1)}, bf16[1,512,768]{1,2,0:T(8,128)(2,1)S(1)}, u32[]{:S(2)}, u32[]{:S(2)}) collective-permute-start(bf16[1,512,768]{1,2,0:T(8,128)(2,1)S(1)} %slice.87), channel_id=1, source_target_pairs={{1,0},{3,2},{5,4},{7,6},{9,8},{11,10},{13,12},{15,14},{17,16},{19,... | collective-permute-start | bytes 2359304 | tf_op jit(solution)/shard_map/while/body/eval_jaxpr/ppermute | solution.py:14
  492.3 96.5 %copy-start.21 = (s32[1024]{0:T(1024)}, s32[1024]{0:T(1024)S(1)}, u32[]{:S(2)}) copy-start(s32[1024]{0:T(1024)S(1)} %get-tuple-element.1068) | copy-start | bytes 12292 | tf_op jit(solution)/shard_map/while
  492.4 96.5 %copy-start.41 = (pred[1024]{0:T(1024)(128)(4,1)}, pred[1024]{0:T(1024)(128)(4,1)S(1)}, u32[]{:S(2)}) copy-start(pred[1024]{0:T(1024)(128)(4,1)S(1)} %get-tuple-element.1069) | copy-start | bytes 3076 | tf_op jit(solution)/shard_map/while
  492.4 72.6 %all-gather.11.cloned.1.call-start = ((), (), s32[]{:S(2)}) async-start(), calls=%async_computation.11 | async-start | bytes 4423680 | tf_op jit(solution)/shard_map/while/body/eval_jaxpr/all_gather | solution.py:114
  493.0 143.5 %all-gather.9.cloned.1.call-start = ((), (), s32[]{:S(2)}) async-start(), calls=%async_computation.10 | async-start | bytes 1474560 | tf_op jit(solution)/shard_map/while/body/eval_jaxpr/all_gather | solution.py:117
  493.6 192.6 %all-gather.13.cloned.1.call-start = ((), (), s32[]{:S(2)}) async-start(), calls=%async_computation.12 | async-start | bytes 5898240 | tf_op jit(solution)/shard_map/while/body/eval_jaxpr/all_gather | solution.py:123
  494.3 281.4 %all-gather.15.cloned.1.call-start = ((), (), s32[]{:S(2)}) async-start(), calls=%async_computation.13 | async-start | bytes 5898240 | tf_op jit(solution)/shard_map/while/body/eval_jaxpr/all_gather | solution.py:163
  569.5 21.7 %collective-permute-start = (bf16[1,512,768]{2,1,0:T(8,128)(2,1)S(1)}, bf16[1,512,768]{2,1,0:T(8,128)(2,1)}, u32[]{:S(2)}, u32[]{:S(2)}) collective-permute-start(bf16[1,512,768]{2,1,0:T(8,128)(2,1)S(1)} %get-tuple-element.924), channel_id=1, source_target_pairs={{0,1},{2,3},{4,5},{6,7},{8,9},{10,11},{12,13},{14,15},{16,17},{18,... | collective-permute-start | bytes 2359304 | tf_op jit(solution)/shard_map/while/body/eval_jaxpr/ppermute | solution.py:14
  573.2 20.3 %collective-permute-start.1 = (bf16[1,512,768]{2,1,0:T(8,128)(2,1)}, bf16[1,512,768]{2,1,0:T(8,128)(2,1)}, u32[]{:S(2)}, u32[]{:S(2)}) collective-permute-start(bf16[1,512,768]{2,1,0:T(8,128)(2,1)} %slice.85), channel_id=1, source_target_pairs={{0,1},{2,3},{4,5},{6,7},{8,9},{10,11},{12,13},{14,15},{16,17},{18,... | collective-permute-start | bytes 2359304 | tf_op jit(solution)/shard_map/while/body/eval_jaxpr/ppermute | solution.py:14
  593.5 30.9 %copy-start = (bf16[1,1024,768]{1,2,0:T(8,128)(2,1)}, bf16[1,1024,768]{1,2,0:T(8,128)(2,1)S(1)}, u32[]{:S(2)}) copy-start(bf16[1,1024,768]{1,2,0:T(8,128)(2,1)S(1)} %copy.50) | copy-start | bytes 4718596 | tf_op jit(solution)/shard_map/while
  639.5 136.2 %copy-start.13 = (bf16[2,1,512,768]{3,2,1,0:T(8,128)(2,1)S(1)}, bf16[2,1,512,768]{3,2,1,0:T(8,128)(2,1)}, u32[]{:S(2)}) copy-start(bf16[2,1,512,768]{3,2,1,0:T(8,128)(2,1)} %get-tuple-element.1058) | copy-start | bytes 4718596 | tf_op jit(solution)/shard_map/while
  939.6 22.8 %collective-permute-start.2 = (bf16[1,512,768]{1,2,0:T(8,128)(2,1)}, bf16[1,512,768]{1,2,0:T(8,128)(2,1)}, u32[]{:S(2)}, u32[]{:S(2)}) collective-permute-start(bf16[1,512,768]{1,2,0:T(8,128)(2,1)} %slice.86), channel_id=1, source_target_pairs={{1,0},{3,2},{5,4},{7,6},{9,8},{11,10},{13,12},{15,14},{17,16},{19,... | collective-permute-start | bytes 2359304 | tf_op jit(solution)/shard_map/while/body/eval_jaxpr/ppermute | solution.py:14
  950.3 14.9 %collective-permute-start.3 = (bf16[1,512,768]{1,2,0:T(8,128)(2,1)S(1)}, bf16[1,512,768]{1,2,0:T(8,128)(2,1)S(1)}, u32[]{:S(2)}, u32[]{:S(2)}) collective-permute-start(bf16[1,512,768]{1,2,0:T(8,128)(2,1)S(1)} %slice.87), channel_id=1, source_target_pairs={{1,0},{3,2},{5,4},{7,6},{9,8},{11,10},{13,12},{15,14},{17,16},{19,... | collective-permute-start | bytes 2359304 | tf_op jit(solution)/shard_map/while/body/eval_jaxpr/ppermute | solution.py:14
  983.9 32.7 %reduce-scatter.7.cloned.1.call-start = ((), (), s32[]{:S(2)}) async-start(), calls=%async_computation.5 | async-start | bytes 1474560 | tf_op jit(solution)/shard_map/reduce_scatter | solution.py:231
  986.8 97.0 %reduce-scatter.5.cloned.1.call-start = ((), (), s32[]{:S(2)}) async-start(), calls=%async_computation.4 | async-start | bytes 4423680 | tf_op jit(solution)/shard_map/reduce_scatter | solution.py:231
  992.0 179.3 %reduce-scatter.9.cloned.1.call-start = ((), (), s32[]{:S(2)}) async-start(), calls=%async_computation.6 | async-start | bytes 5898240 | tf_op jit(solution)/shard_map/reduce_scatter | solution.py:231
  998.8 260.5 %reduce-scatter.11.cloned.1.call-start = ((), (), s32[]{:S(2)}) async-start(), calls=%async_computation.7 | async-start | bytes 5898240 | tf_op jit(solution)/shard_map/reduce_scatter | solution.py:231
  1005.3 281.1 %all-reduce.38.cloned.1.call-start = ((), (), s32[]{:S(2)}) async-start(), calls=%async_computation.9 | async-start | bytes 7077888 | tf_op jit(solution)/shard_map/psum | solution.py:234
  1259.4 29.1 %copy-start.20 = (f32[3072]{0:T(1024)S(1)}, f32[3072]{0:T(1024)}, u32[]{:S(2)}) copy-start(f32[3072]{0:T(1024)} %get-tuple-element.430) | copy-start | bytes 36868
  1259.4 126.3 %all-reduce.36.cloned.1.call-start = ((), (), s32[]{:S(2)}) async-start(), calls=%async_computation.8 | async-start | bytes 7077888 | tf_op jit(solution)/shard_map/psum | solution.py:234
  (81 other events, 594.1 us)
Sparse Core Ops, SparseCore 0:
  11.2 73.1 all-gather.10
  86.0 29.1 all-gather.8
  116.8 88.5 all-gather.12
  206.9 87.8 all-gather.14
  494.6 70.4 all-gather.10
  566.5 29.3 all-gather.8
  597.6 88.5 all-gather.12
  687.8 87.8 all-gather.14
Sparse Core Ops, SparseCore 1:
  987.3 29.2 reduce-scatter.6
  1018.7 65.0 reduce-scatter.4
  1085.9 85.3 reduce-scatter.8
  1173.6 85.6 reduce-scatter.10
  1261.9 24.4 all-reduce.37
  1290.2 95.4 all-reduce.35
